TPU v7x, 32 devices: a whole 2x2x4 slice. The times are simulated.
32 devices in a mesh: pipe: 4 (over y, core), expert: 2 (over x), dp: 4 (over z).
Axes of the slice: x: 2, y: 2, z: 4, core: 2. Of those that a mesh axis runs over, the one named last changes fastest.
Arguments:
- tokens: bfloat16 [4, 1024, 3072], P('pipe', ('expert', 'dp')), may hold values from -6 to 6
- grad_out: bfloat16 [4, 1024, 3072], P('pipe', ('expert', 'dp')), may hold values from -6 to 6
- routes: int32 [4, 1024, 2], P('pipe', ('expert', 'dp')), may hold values from 0 to 7, as said below
- route_weights: float32 [4, 1024, 2], P('pipe', ('expert', 'dp')), may hold values from 0.1 to 0.9
- gate_weight: bfloat16 [4, 3072, 32768], P('pipe', None, ('expert', 'dp')), may hold values from -0.109375 to 0.109375
- up_weight: bfloat16 [4, 3072, 32768], P('pipe', None, ('expert', 'dp')), may hold values from -0.109375 to 0.109375
- down_weight: bfloat16 [4, 32768, 3072], P('pipe', ('expert', 'dp')), may hold values from -0.046875 to 0.046875
Outputs:
- upstream: bfloat16 [4, 1024, 3072], P('pipe', ('expert', 'dp'))
Inputs may be any that keep to these rules, and one draw needn't show every extreme that they name: `routes`: each row names two different experts. In every section, for each window expert e < 2, the tokens of one device that name e number 1 to 8, exactly 8 on some device, and the tokens of the whole section name e exactly 36 times.
All inputs are finite; a program needn't handle non-finite values.
Results may differ from a plain program's by a relative error of at most 0.0013.
Values may be sent and summed in bfloat16 or wider, within the bound.
No kernel may reach another device: no remote copies, remote signals or barrier semaphores. Data moves between devices by JAX's collectives and lax.ppermute only.
A program may use at most 192 MiB of HBM per device.

v0:
```python
import jax
import jax.numpy as jnp
from jax import lax
from jax.sharding import PartitionSpec as P

EF = 2
CAP = 8


def from_behind(value, axis, steps):
    count = lax.axis_size(axis)
    first, last = (max(0, -steps), min(count, count - steps))
    return lax.ppermute(value, axis, [(source, source + steps) for source in range(first, last)])


def hidden_grads(rows_in, rows_grad, gate_slice, up_slice, down_slice):
    gate_pre = jnp.dot(rows_in, gate_slice, preferred_element_type=jnp.float32)
    up_pre = jnp.dot(rows_in, up_slice, preferred_element_type=jnp.float32)
    sigmoid_gate = jax.nn.sigmoid(gate_pre)
    contract = (((1,), (1,)), ((), ()))
    act_grad = lax.dot_general(rows_grad, down_slice, contract, preferred_element_type=jnp.float32)
    gate_grad = (act_grad * up_pre * sigmoid_gate * (1.0 + gate_pre * (1.0 - sigmoid_gate))).astype(
        jnp.bfloat16
    )
    up_grad = (act_grad * gate_pre * sigmoid_gate).astype(jnp.bfloat16)
    result = lax.dot_general(gate_grad, gate_slice, contract, preferred_element_type=jnp.float32)
    return result + lax.dot_general(up_grad, up_slice, contract, preferred_element_type=jnp.float32)


def shards(tokens, grad_out, routes, route_weights, gate_weight, up_weight, down_weight):
    expert_count = lax.axis_size("expert")
    data_count = lax.axis_size("dp")
    device_count = expert_count * data_count
    group_size = device_count // EF
    inputs = tokens[0]
    upstream_grad = grad_out[0]
    picks = routes[0]
    pick_weights = route_weights[0]
    width = inputs.shape[1]
    capacity = CAP
    slot_range = jnp.arange(capacity, dtype=jnp.int32)
    upstream_float = upstream_grad.astype(jnp.float32)
    sent_inputs = []
    sent_grads = []
    sent_counts = []
    chosen_sets = []
    slot_places = []
    for expert in range(EF):
        first_pick = picks[:, 0] == expert
        second_pick = picks[:, 1] == expert
        chosen = first_pick | second_pick
        weight = jnp.where(first_pick, pick_weights[:, 0], 0.0) + jnp.where(
            second_pick, pick_weights[:, 1], 0.0
        )
        slot_place = jnp.cumsum(chosen.astype(jnp.int32)) - 1
        slot_table = ((slot_place[None, :] == slot_range[:, None]) & chosen[None, :]).astype(
            jnp.bfloat16
        )
        scaled = (weight[:, None] * upstream_float).astype(jnp.bfloat16)
        sent_inputs.append(
            jnp.dot(slot_table, inputs, preferred_element_type=jnp.float32).astype(jnp.bfloat16)
        )
        sent_grads.append(
            jnp.dot(slot_table, scaled, preferred_element_type=jnp.float32).astype(jnp.bfloat16)
        )
        sent_counts.append(jnp.sum(chosen.astype(jnp.int32)))
        chosen_sets.append(chosen)
        slot_places.append(jnp.clip(slot_place, 0, capacity - 1))
    stack_inputs = jnp.stack(sent_inputs)
    stack_grads = jnp.stack(sent_grads)
    stack_counts = jnp.stack(sent_counts)
    bound_inputs = jnp.repeat(stack_inputs, group_size, axis=0)
    bound_grads = jnp.repeat(stack_grads, group_size, axis=0)
    bound_counts = jnp.repeat(stack_counts, group_size)[:, None]
    recv_inputs, recv_grads, recv_counts = (
        lax.all_to_all(bound_inputs, ("expert", "dp"), split_axis=0, concat_axis=0, tiled=True),
        lax.all_to_all(bound_grads, ("expert", "dp"), split_axis=0, concat_axis=0, tiled=True),
        lax.all_to_all(bound_counts, ("expert", "dp"), split_axis=0, concat_axis=0, tiled=True),
    )
    rows_in = recv_inputs.reshape(device_count * capacity, width)
    rows_grad = recv_grads.reshape(device_count * capacity, width)
    counts_in = recv_counts[:, 0]
    live_slots = (slot_range[None, :] < counts_in[:, None]).reshape(-1)
    gate_slice = gate_weight[0]
    up_slice = up_weight[0]
    down_slice = down_weight[0]
    partial_value = hidden_grads(rows_in, rows_grad, gate_slice, up_slice, down_slice) * live_slots[
        :, None
    ].astype(jnp.float32)
    partial_bf = partial_value.astype(jnp.bfloat16).reshape(device_count, capacity, width)
    returned = lax.all_to_all(partial_bf, ("expert", "dp"), split_axis=0, concat_axis=0, tiled=True)
    summed = returned.astype(jnp.float32).reshape(EF, group_size, capacity, width).sum(axis=1)
    branch = jnp.zeros_like(upstream_float)
    for expert in range(EF):
        picked_rows = summed[expert][slot_places[expert]]
        branch = branch + jnp.where(chosen_sets[expert][:, None], picked_rows, 0.0)
    grad_in = (upstream_float + branch).astype(jnp.bfloat16)[None]
    return from_behind(grad_in, "pipe", -1)


def solution(mesh):
    placed = (
        P("pipe", ("expert", "dp"), None),
        P("pipe", ("expert", "dp"), None),
        P("pipe", ("expert", "dp"), None),
        P("pipe", ("expert", "dp"), None),
        P("pipe", None, ("expert", "dp")),
        P("pipe", None, ("expert", "dp")),
        P("pipe", ("expert", "dp"), None),
    )
    return jax.shard_map(
        shards,
        mesh=mesh,
        in_specs=placed,
        out_specs=P("pipe", ("expert", "dp"), None),
        check_vma=False,
    )
```

profile of v0, /device:TPU:1, one launch (start us, length us, event | category | flops | bytes accessed | tf_op | source)
XLA Modules:
  0.0 130.9 jit_solution(7416122396753780305)
XLA Ops:
  0.0 0.0 copy-start
  0.0 0.0 copy-start.2
  0.0 0.9 copy.15
  0.9 0.2 or_reduce_fusion
  1.1 0.7 convert_reduce_fusion.1
  1.8 1.4 %pad_add_fusion = s32[2]{0:T(128)S(1)} fusion(s32[1]{0:T(128)} %bitcast.16, s32[1]{0:T(128)} %bitcast.15), kind=kLoop, calls=%fused_computation.89 | loop fusion | flops 2 | bytes 16 | tf_op jit(solution)/shard_map/stack | solution.py:71
  3.2 0.1 broadcast_in_dim.55
  3.3 0.7 all_to_all.20
  4.0 6.4 %all-to-all-start.2 = ((s32[8,1,1]{2,1,0:T(1,128)}), s32[8,1,1]{2,1,0:T(1,128)S(1)}, u32[]{:S(2)}, u32[]{:S(2)}) async-start(s32[8,1,1]{2,1,0:T(1,128)} %all_to_all.20), calls=%async_computation.2 | async-start | bytes 8192 | tf_op jit(solution)/shard_map/all_to_all | solution.py:78
  10.3 0.8 copy.16
  11.1 0.2 add_reduce_fusion.1
  11.3 0.2 reduce-window.9
  11.5 0.1 fusion.70
  11.6 0.2 reduce-window.6
  11.8 0.1 fusion.69
  11.9 1.4 %fusion.44 = bf16[1,8,3072]{2,1,0:T(8,128)(2,1)S(1)} fusion(bf16[1,128,3072]{2,1,0:T(8,128)(2,1)} %param.8, f32[128]{0:T(128)S(1)} %get-tuple-element.9, s32[128]{0:T(128)S(1)} %get-tuple-element.6, pred[128]{0:T(512)(128)(4,1)S(1)} %get-tuple-element.19), kind=kOutput, calls=%fused_computation.24 | convolution fusion | flops 7497728 | bytes 836736 | tf_op jit(solution)/shard_map/dot_general | solution.py:64
  13.3 0.0 copy-done.2
  13.4 0.3 fusion.45
  13.7 0.0 copy-done
  13.7 0.2 fusion.46
  13.9 1.7 %all-to-all-done.2 = s32[8,1,1]{2,1,0:T(1,128)S(1)} async-done(((s32[8,1,1]{2,1,0:T(1,128)}), s32[8,1,1]{2,1,0:T(1,128)S(1)}, u32[]{:S(2)}, u32[]{:S(2)}) %all-to-all-start.2) | async-done | bytes 64 | tf_op jit(solution)/shard_map/all_to_all | solution.py:78
  15.6 0.8 broadcast_in_dim.53
  16.3 3.8 %all-to-all-start = ((bf16[8,8,3072]{2,1,0:T(8,128)(2,1)}), bf16[8,8,3072]{2,1,0:T(8,128)(2,1)S(1)}, u32[]{:S(2)}, u32[]{:S(2)}) async-start(bf16[8,8,3072]{2,1,0:T(8,128)(2,1)} %bitcast.5), calls=%async_computation | async-start | bytes 786432 | tf_op jit(solution)/shard_map/all_to_all | solution.py:77
  20.1 0.2 fusion.47
  20.4 0.2 reduce.6
  20.6 0.1 fusion.77
  20.7 0.1 reshape.211
  20.8 8.8 %all-to-all-done = bf16[8,8,3072]{2,1,0:T(8,128)(2,1)S(1)} async-done(((bf16[8,8,3072]{2,1,0:T(8,128)(2,1)}), bf16[8,8,3072]{2,1,0:T(8,128)(2,1)S(1)}, u32[]{:S(2)}, u32[]{:S(2)}) %all-to-all-start) | async-done | bytes 393248 | tf_op jit(solution)/shard_map/all_to_all | solution.py:77
  29.6 0.8 broadcast_in_dim.54
  30.4 5.2 %all-to-all-start.1 = ((bf16[8,8,3072]{2,1,0:T(8,128)(2,1)}), bf16[8,8,3072]{2,1,0:T(8,128)(2,1)S(1)}, u32[]{:S(2)}, u32[]{:S(2)}) async-start(bf16[8,8,3072]{2,1,0:T(8,128)(2,1)} %bitcast.11), calls=%async_computation.1 | async-start | bytes 786432 | tf_op jit(solution)/shard_map/all_to_all | solution.py:76
  35.6 12.4 %fusion.8 = f32[64,4096]{1,0:T(8,128)S(1)} fusion(bf16[1,4096,3072]{2,1,0:T(8,128)(2,1)} %param.13, bf16[8,8,3072]{2,1,0:T(8,128)(2,1)S(1)} %all-to-all-done), kind=kOutput, calls=%fused_computation.10 | convolution fusion | flops 1610612736 | bytes 26607616 | tf_op jit(solution)/shard_map/dot_general | solution.py:21
  48.0 0.0 all-to-all-done.1
  48.1 10.5 %fusion.2 = f32[64,4096]{1,0:T(8,128)S(1)} fusion(bf16[1,3072,4096]{2,1,0:T(8,128)(2,1)} %param.11, bf16[8,8,3072]{2,1,0:T(8,128)(2,1)S(1)} %all-to-all-done.1), kind=kOutput, calls=%fused_computation.4 | convolution fusion | flops 1610612736 | bytes 26607616 | tf_op jit(solution)/shard_map/dot_general | solution.py:17
  58.5 13.3 %fusion.4 = f32[64,3072]{1,0:T(8,128)} fusion(bf16[1,3072,4096]{2,1,0:T(8,128)(2,1)} %param.12, f32[64,4096]{1,0:T(8,128)S(1)} %fusion.8, f32[64,4096]{1,0:T(8,128)S(1)} %fusion.2), kind=kOutput, calls=%fused_computation.6 | convolution fusion | flops 1612185600 | bytes 28049408 | tf_op jit(solution)/shard_map/dot_general | solution.py:27
  71.8 20.9 %fusion.39 = bf16[8,8,3072]{2,1,0:T(8,128)(2,1)} fusion(f32[64,3072]{1,0:T(8,128)} %fusion.4, bf16[1,3072,4096]{2,1,0:T(8,128)(2,1)} %param.11, f32[64,4096]{1,0:T(8,128)S(1)} %fusion.8, bf16[1,3072,4096]{2,1,0:T(8,128)(2,1)} %param.12, f32[64,4096]{1,0:T(8,128)S(1)} %fusion.2, bf16[8,8,3072]{2,1,0:T(8,128)(2,1)S(1)} %all-to-all-done.1, f32[64]{0:T(128)S(1)} %reshape.211), kind=kOutput, calls=%fused_computation.19 | convolution fusion | flops 3224436736 | bytes 54001920 | tf_op jit(solution)/shard_map/dot_general | solution.py:26
  92.8 5.4 %all-to-all-start.3 = ((bf16[8,8,3072]{2,1,0:T(8,128)(2,1)}), bf16[8,8,3072]{2,1,0:T(8,128)(2,1)S(1)}, u32[]{:S(2)}, u32[]{:S(2)}) async-start(bf16[8,8,3072]{2,1,0:T(8,128)(2,1)} %fusion.39), calls=%async_computation.3 | async-start | bytes 786432 | tf_op jit(solution)/shard_map/all_to_all | solution.py:91
  98.2 8.7 %all-to-all-done.3 = bf16[8,8,3072]{2,1,0:T(8,128)(2,1)S(1)} async-done(((bf16[8,8,3072]{2,1,0:T(8,128)(2,1)}), bf16[8,8,3072]{2,1,0:T(8,128)(2,1)S(1)}, u32[]{:S(2)}, u32[]{:S(2)}) %all-to-all-start.3) | async-done | bytes 393248 | tf_op jit(solution)/shard_map/all_to_all | solution.py:91
  107.0 1.2 gather_fusion
  108.2 0.0 copy-start.3
  108.2 2.3 %gather_fusion.1 = f32[128,3072]{1,0:T(8,128)} fusion(f32[8,3072]{1,0:T(8,128)S(1)} %get-tuple-element.18, s32[1024]{0:T(1024)S(1)} %pad_clamp_fusion), kind=kCustom, calls=%fused_computation.1 | custom fusion | bytes 3146240 | tf_op jit(solution)/shard_map/gather | solution.py:95
  110.5 0.0 copy-done.3
  110.5 0.0 copy-start.1
  110.5 1.9 %fusion.52 = bf16[1,128,3072]{2,1,0:T(8,128)(2,1)S(1)} fusion(bf16[1,128,3072]{2,1,0:T(8,128)(2,1)S(1)} %copy-done.3, f32[128,3072]{1,0:T(8,128)} %gather_fusion.1, f32[128,3072]{1,0:T(8,128)S(1)} %gather_fusion, pred[128]{0:T(512)(128)(4,1)S(1)} %get-tuple-element.14, pred[128]{0:T(512)(128)(4,1)S(1)} %get-tuple-element.19), kind=kLoop, calls=%fused_computation.34 | loop fusion | flops 2359296 | bytes 4718848 | tf_op jit(solution)/shard_map/convert_element_type | solution.py:97
  112.4 6.8 %collective-permute-start = (bf16[1,128,3072]{2,1,0:T(8,128)(2,1)S(1)}, bf16[1,128,3072]{2,1,0:T(8,128)(2,1)S(1)}, u32[]{:S(2)}, u32[]{:S(2)}) collective-permute-start(bf16[1,128,3072]{2,1,0:T(8,128)(2,1)S(1)} %fusion.52), channel_id=1, source_target_pairs={{8,0},{16,8},{24,16},{9,1},{17,9},{25,17},{10,2},{18,10},{26,18},{... | collective-permute-start | bytes 2359304 | tf_op jit(solution)/shard_map/ppermute | solution.py:13
  119.2 10.8 %collective-permute-done = bf16[1,128,3072]{2,1,0:T(8,128)(2,1)S(1)} collective-permute-done((bf16[1,128,3072]{2,1,0:T(8,128)(2,1)S(1)}, bf16[1,128,3072]{2,1,0:T(8,128)(2,1)S(1)}, u32[]{:S(2)}, u32[]{:S(2)}) %collective-permute-start) | collective-permute-done | bytes 786464 | tf_op jit(solution)/shard_map/ppermute | solution.py:13
  130.0 0.9 copy.19
  130.9 0.0 copy-done.1
  (7 shorter events, 0.1 us)
Async XLA Ops:
  0.0 13.7 %copy-start = (bf16[1,128,3072]{2,1,0:T(8,128)(2,1)S(1)}, bf16[1,128,3072]{2,1,0:T(8,128)(2,1)}, u32[]{:S(2)}) copy-start(bf16[1,128,3072]{2,1,0:T(8,128)(2,1)} %param.7) | copy-start | bytes 2359300
  0.0 13.3 %copy-start.2 = (bf16[1,128,3072]{2,1,0:T(8,128)(2,1)S(1)}, bf16[1,128,3072]{2,1,0:T(8,128)(2,1)}, u32[]{:S(2)}) copy-start(bf16[1,128,3072]{2,1,0:T(8,128)(2,1)} %param.8) | copy-start | bytes 2359300
  4.0 11.6 %all-to-all-start.2 = ((s32[8,1,1]{2,1,0:T(1,128)}), s32[8,1,1]{2,1,0:T(1,128)S(1)}, u32[]{:S(2)}, u32[]{:S(2)}) async-start(s32[8,1,1]{2,1,0:T(1,128)} %all_to_all.20), calls=%async_computation.2 | async-start | bytes 8192 | tf_op jit(solution)/shard_map/all_to_all | solution.py:78
  16.3 13.3 %all-to-all-start = ((bf16[8,8,3072]{2,1,0:T(8,128)(2,1)}), bf16[8,8,3072]{2,1,0:T(8,128)(2,1)S(1)}, u32[]{:S(2)}, u32[]{:S(2)}) async-start(bf16[8,8,3072]{2,1,0:T(8,128)(2,1)} %bitcast.5), calls=%async_computation | async-start | bytes 786432 | tf_op jit(solution)/shard_map/all_to_all | solution.py:77
  30.4 17.7 %all-to-all-start.1 = ((bf16[8,8,3072]{2,1,0:T(8,128)(2,1)}), bf16[8,8,3072]{2,1,0:T(8,128)(2,1)S(1)}, u32[]{:S(2)}, u32[]{:S(2)}) async-start(bf16[8,8,3072]{2,1,0:T(8,128)(2,1)} %bitcast.11), calls=%async_computation.1 | async-start | bytes 786432 | tf_op jit(solution)/shard_map/all_to_all | solution.py:76
  92.8 14.2 %all-to-all-start.3 = ((bf16[8,8,3072]{2,1,0:T(8,128)(2,1)}), bf16[8,8,3072]{2,1,0:T(8,128)(2,1)S(1)}, u32[]{:S(2)}, u32[]{:S(2)}) async-start(bf16[8,8,3072]{2,1,0:T(8,128)(2,1)} %fusion.39), calls=%async_computation.3 | async-start | bytes 786432 | tf_op jit(solution)/shard_map/all_to_all | solution.py:91
  108.2 2.3 %copy-start.3 = (bf16[1,128,3072]{2,1,0:T(8,128)(2,1)S(1)}, bf16[1,128,3072]{2,1,0:T(8,128)(2,1)}, u32[]{:S(2)}) copy-start(bf16[1,128,3072]{2,1,0:T(8,128)(2,1)} %param.8) | copy-start | bytes 2359300
  110.5 20.4 %copy-start.1 = (bf16[1,128,3072]{2,1,0:T(8,128)(2,1)S(1)}, bf16[1,128,3072]{2,1,0:T(8,128)(2,1)}, u32[]{:S(2)}) copy-start(bf16[1,128,3072]{2,1,0:T(8,128)(2,1)} %param.7) | copy-start | bytes 2359300
  112.4 17.6 %collective-permute-start = (bf16[1,128,3072]{2,1,0:T(8,128)(2,1)S(1)}, bf16[1,128,3072]{2,1,0:T(8,128)(2,1)S(1)}, u32[]{:S(2)}, u32[]{:S(2)}) collective-permute-start(bf16[1,128,3072]{2,1,0:T(8,128)(2,1)S(1)} %fusion.52), channel_id=1, source_target_pairs={{8,0},{16,8},{24,16},{9,1},{17,9},{25,17},{10,2},{18,10},{26,18},{... | collective-permute-start | bytes 2359304 | tf_op jit(solution)/shard_map/ppermute | solution.py:13
where the time goes:
time: 131 us
  matrix products  59.3 us (45%)
  waiting for transfers between devices  30 us (23%)
  starting transfers between devices  27.5 us (21%)
  local copies, waits for them, and re-layouts  8.41 us (6%)
  other arithmetic  5.42 us (4%)
    dot_general x1, matrix products, hidden_grads(): lax.dot_general(gate_grad, gate_slice, contract, preferred_element_type=j...  20.9 us
    dot_general x1, matrix products, hidden_grads(): lax.dot_general(up_grad, up_slice, contract, preferred_element_type=jnp.f...  13.3 us
    dot_general x1, matrix products, hidden_grads(): lax.dot_general(rows_grad, down_slice, contract, preferred_element_type=j...  12.4 us
    ppermute x1, waiting for transfers between devices, from_behind(): lax.ppermute(value, axis, [(source, source + steps) for source in range(f...  10.8 us
    dot_general x1, matrix products, hidden_grads(): gate_pre = jnp.dot(rows_in, gate_slice, preferred_element_type=jnp.float32)  10.5 us
    all_to_all x1, waiting for transfers between devices, shards(): lax.all_to_all(bound_grads, ('expert', 'dp'), split_axis=0, concat_axis=0...  8.85 us
    all_to_all x1, waiting for transfers between devices, shards(): lax.all_to_all(partial_bf, ('expert', 'dp'), split_axis=0, concat_axis=0,...  8.71 us
    ppermute x1, starting transfers between devices, from_behind(): lax.ppermute(value, axis, [(source, source + steps) for source in range(f...  6.76 us
  transfers between devices with their start and end apart: 5, of which 4 were waited for; matrix products, arithmetic and copies ran while one was open for 13% of the time, Pallas kernels for 0%

commit v1 on v0

--- a/solution.py
+++ b/solution.py
@@ -1,3 +1,4 @@
+import functools
 import jax
 import jax.numpy as jnp
 from jax import lax
@@ -5,6 +6,46 @@
 
 EF = 2
 CAP = 8
+
+
+def spread_field(z_in, join_dim, array_here):
+    state_next = z_in.shape
+    carry_in = z_in.reshape(
+        *state_next[:join_dim],
+        array_here,
+        state_next[join_dim] // array_here,
+        *state_next[join_dim + 1 :]
+    )
+    return jnp.moveaxis(carry_in, join_dim, 0)
+
+
+def read_patches_in(point, d0):
+    point = jnp.moveaxis(point, 0, d0)
+    passed = point.shape
+    return point.reshape(*passed[:d0], passed[d0] * passed[d0 + 1], *passed[d0 + 2 :])
+
+
+def panel_use(raw, mesh_name, unit, my_tile):
+    plain = lax.axis_size(mesh_name)
+    raw_out, outcome_arr = (plain, lax.axis_index(mesh_name))
+    v1 = spread_field(raw, unit, raw_out)
+    row_out = v1
+    d = 1
+    while d < raw_out:
+        oldest, wide_out = ((outcome_arr + d) % raw_out, (outcome_arr - d) % raw_out)
+        fresh = lax.dynamic_index_in_dim(v1, oldest, 0)
+        ledger = []
+        rr = 0
+        while rr < raw_out:
+            ledger.append((rr, (rr + d) % raw_out))
+            rr += 1
+        v_next = lax.ppermute(fresh, axis_name=mesh_name, perm=ledger)
+        row_out = lax.dynamic_update_slice_in_dim(row_out, v_next, wide_out, axis=0)
+        d += 1
+    return read_patches_in(row_out, my_tile)
+
+
+end_lots_all = functools.partial(panel_use, mesh_name=("expert", "dp"), unit=0, my_tile=0)
 
 
 def from_behind(value, axis, steps):
@@ -73,7 +114,7 @@
     bound_grads = jnp.repeat(stack_grads, group_size, axis=0)
     bound_counts = jnp.repeat(stack_counts, group_size)[:, None]
     recv_inputs, recv_grads, recv_counts = (
-        lax.all_to_all(bound_inputs, ("expert", "dp"), split_axis=0, concat_axis=0, tiled=True),
+        end_lots_all(bound_inputs),
         lax.all_to_all(bound_grads, ("expert", "dp"), split_axis=0, concat_axis=0, tiled=True),
         lax.all_to_all(bound_counts, ("expert", "dp"), split_axis=0, concat_axis=0, tiled=True),
     )

time: 131 us -> 134 us (1.023)
  starting transfers between devices: 27.5 us -> 35.8 us
  waiting for transfers between devices: 30 us -> 26.6 us
  local copies, waits for them, and re-layouts: 8.41 us -> 7.06 us
    ppermute x0 -> x7, starting transfers between devices: none -> 13.7 us  [panel_use(): v_next = lax.ppermute(fresh, axis_name=mesh_name, perm=ledger)]
    all_to_all x1, waiting for transfers between devices: 8.85 us -> 0.01 us  [shards(): lax.all_to_all(bound_grads, ('expert', 'dp'), split_axis=0, concat_axis=0...]
    ppermute x0 -> x7, waiting for transfers between devices: none -> 5.75 us  [panel_use(): v_next = lax.ppermute(fresh, axis_name=mesh_name, perm=ledger)]
    all_to_all x1 -> x0, starting transfers between devices: 5.21 us -> none  [shards(): lax.all_to_all(bound_inputs, ('expert', 'dp'), split_axis=0, concat_axis=...]
  transfers between devices with their start and end apart: 5 -> 11, of which waited for: 4 -> 5; matrix products, arithmetic and copies ran while one was open for 13% -> 10% of each run, Pallas kernels for 0% -> 0%
where the time goes in v1:
time: 134 us
  matrix products  58.2 us (43%)
  starting transfers between devices  35.8 us (27%)
  waiting for transfers between devices  26.6 us (20%)
  local copies, waits for them, and re-layouts  7.06 us (5%)
  other arithmetic  5.4 us (4%)
    dot_general x1, matrix products, hidden_grads(): lax.dot_general(gate_grad, gate_slice, contract, preferred_element_type=j...  20.9 us
    ppermute x7, starting transfers between devices, panel_use(): v_next = lax.ppermute(fresh, axis_name=mesh_name, perm=ledger)  13.7 us
    dot_general x1, matrix products, hidden_grads(): lax.dot_general(up_grad, up_slice, contract, preferred_element_type=jnp.f...  13.3 us
    dot_general x1, matrix products, hidden_grads(): lax.dot_general(rows_grad, down_slice, contract, preferred_element_type=j...  12.4 us
    ppermute x1, waiting for transfers between devices, from_behind(): lax.ppermute(value, axis, [(source, source + steps) for source in range(f...  10.8 us
    dot_general x1, matrix products, hidden_grads(): gate_pre = jnp.dot(rows_in, gate_slice, preferred_element_type=jnp.float32)  10.5 us
    all_to_all x1, waiting for transfers between devices, shards(): lax.all_to_all(partial_bf, ('expert', 'dp'), split_axis=0, concat_axis=0,...  8.68 us
    ppermute x1, starting transfers between devices, from_behind(): lax.ppermute(value, axis, [(source, source + steps) for source in range(f...  6.99 us
  transfers between devices with their start and end apart: 11, of which 5 were waited for; matrix products, arithmetic and copies ran while one was open for 10% of the time, Pallas kernels for 0%

profile of v1, /device:TPU:1, one launch (start us, length us, event | category | flops | bytes accessed | tf_op | source)
XLA Modules:
  0.0 133.6 jit_solution(15699210228304034011)
XLA Ops:
  0.0 0.9 copy.15
  0.9 0.2 or_reduce_fusion
  1.0 0.0 copy-start.4
  1.1 0.7 convert_reduce_fusion.1
  1.8 1.4 %pad_add_fusion = s32[2]{0:T(128)S(1)} fusion(s32[1]{0:T(128)} %bitcast.16, s32[1]{0:T(128)} %bitcast.15), kind=kLoop, calls=%fused_computation.103 | loop fusion | flops 2 | bytes 16 | tf_op jit(solution)/shard_map/stack | solution.py:112
  3.2 0.1 broadcast_in_dim.55
  3.3 0.7 all_to_all.16
  3.9 6.4 %all-to-all-start.1 = ((s32[8,1,1]{2,1,0:T(1,128)}), s32[8,1,1]{2,1,0:T(1,128)S(1)}, u32[]{:S(2)}, u32[]{:S(2)}) async-start(s32[8,1,1]{2,1,0:T(1,128)} %all_to_all.16), calls=%async_computation.1 | async-start | bytes 8192 | tf_op jit(solution)/shard_map/all_to_all | solution.py:119
  10.3 0.0 copy-start.2
  10.3 0.2 reduce-window.9
  10.5 0.1 fusion.70
  10.6 0.2 reduce-window.6
  10.8 0.1 fusion.69
  10.9 0.2 fusion.46
  11.1 0.2 fusion.47
  11.4 1.5 %collective-permute-start = (bf16[1,1,8,3072]{3,2,0,1:T(8,128)(2,1)S(1)}, bf16[1,1,8,3072]{3,2,0,1:T(8,128)(2,1)S(1)}, u32[]{:S(2)}, u32[]{:S(2)}) collective-permute-start(bf16[1,1,8,3072]{3,2,0,1:T(8,128)(2,1)S(1)} %constant_dynamic-slice_fusion.6), channel_id=1, source_target_pairs={{0,1},{1,2},{2,3},{3,4},{4,5},{5,6},{6,7},{7,0},{8,9},{9,10},{10,1... | collective-permute-start | bytes 147464 | tf_op jit(solution)/shard_map/ppermute | solution.py:42
  12.9 0.1 copy.16
  13.0 0.2 add_reduce_fusion.1
  13.2 0.3 fusion.44
  13.5 0.3 fusion.45
  14.1 1.4 %all-to-all-done.1 = s32[8,1,1]{2,1,0:T(1,128)S(1)} async-done(((s32[8,1,1]{2,1,0:T(1,128)}), s32[8,1,1]{2,1,0:T(1,128)S(1)}, u32[]{:S(2)}, u32[]{:S(2)}) %all-to-all-start.1) | async-done | bytes 64 | tf_op jit(solution)/shard_map/all_to_all | solution.py:119
  15.5 0.8 broadcast_in_dim.53
  16.3 3.5 %all-to-all-start = ((bf16[8,8,3072]{2,1,0:T(8,128)(2,1)}), bf16[8,8,3072]{2,1,0:T(8,128)(2,1)S(1)}, u32[]{:S(2)}, u32[]{:S(2)}) async-start(bf16[8,8,3072]{2,1,0:T(8,128)(2,1)} %bitcast.5), calls=%async_computation | async-start | bytes 786432 | tf_op jit(solution)/shard_map/all_to_all | solution.py:118
  19.8 0.2 reduce.6
  20.0 0.0 collective-permute-done
  20.1 2.3 %collective-permute-start.1 = (bf16[1,1,8,3072]{3,2,0,1:T(8,128)(2,1)S(1)}, bf16[1,1,8,3072]{3,2,0,1:T(8,128)(2,1)S(1)}, u32[]{:S(2)}, u32[]{:S(2)}) collective-permute-start(bf16[1,1,8,3072]{3,2,0,1:T(8,128)(2,1)S(1)} %get-tuple-element.22), channel_id=1, source_target_pairs={{0,2},{1,3},{2,4},{3,5},{4,6},{5,7},{6,0},{7,1},{8,10},{9,11},{10,... | collective-permute-start | bytes 147464 | tf_op jit(solution)/shard_map/ppermute | solution.py:42
  22.4 0.1 fusion.77
  22.4 0.1 reshape.203
  22.5 2.1 %collective-permute-start.6 = (bf16[1,1,8,3072]{3,2,0,1:T(8,128)(2,1)S(1)}, bf16[1,1,8,3072]{3,2,0,1:T(8,128)(2,1)S(1)}, u32[]{:S(2)}, u32[]{:S(2)}) collective-permute-start(bf16[1,1,8,3072]{3,2,0,1:T(8,128)(2,1)S(1)} %get-tuple-element.17), channel_id=1, source_target_pairs={{0,7},{1,0},{2,1},{3,2},{4,3},{5,4},{6,5},{7,6},{8,15},{9,8},{10,9... | collective-permute-start | bytes 147464 | tf_op jit(solution)/shard_map/ppermute | solution.py:42
  24.6 1.2 collective-permute-start.5
  25.8 0.3 collective-permute-start.4
  26.1 0.1 collective-permute-start.3
  26.2 3.8 %collective-permute-done.1 = bf16[1,1,8,3072]{3,2,0,1:T(8,128)(2,1)S(1)} collective-permute-done((bf16[1,1,8,3072]{3,2,0,1:T(8,128)(2,1)S(1)}, bf16[1,1,8,3072]{3,2,0,1:T(8,128)(2,1)S(1)}, u32[]{:S(2)}, u32[]{:S(2)}) %collective-permute-start.1) | collective-permute-done | bytes 49184 | tf_op jit(solution)/shard_map/ppermute | solution.py:42
  30.0 6.2 %collective-permute-start.2 = (bf16[1,1,8,3072]{3,2,0,1:T(8,128)(2,1)S(1)}, bf16[1,1,8,3072]{3,2,0,1:T(8,128)(2,1)S(1)}, u32[]{:S(2)}, u32[]{:S(2)}) collective-permute-start(bf16[1,1,8,3072]{3,2,0,1:T(8,128)(2,1)S(1)} %get-tuple-element.21), channel_id=1, source_target_pairs={{0,3},{1,4},{2,5},{3,6},{4,7},{5,0},{6,1},{7,2},{8,11},{9,12},{10,... | collective-permute-start | bytes 147464 | tf_op jit(solution)/shard_map/ppermute | solution.py:42
  36.2 1.9 %collective-permute-done.2 = bf16[1,1,8,3072]{3,2,0,1:T(8,128)(2,1)S(1)} collective-permute-done((bf16[1,1,8,3072]{3,2,0,1:T(8,128)(2,1)S(1)}, bf16[1,1,8,3072]{3,2,0,1:T(8,128)(2,1)S(1)}, u32[]{:S(2)}, u32[]{:S(2)}) %collective-permute-start.2) | collective-permute-done | bytes 49184 | tf_op jit(solution)/shard_map/ppermute | solution.py:42
  38.3 10.5 %fusion.2 = f32[64,4096]{1,0:T(8,128)S(1)} fusion(bf16[1,3072,4096]{2,1,0:T(8,128)(2,1)} %param.11, bf16[8,1,8,3072]{3,2,0,1:T(8,128)(2,1)S(1)} %constant_dynamic-update-slice_fusion), kind=kOutput, calls=%fused_computation.4 | convolution fusion | flops 1610612736 | bytes 26607616 | tf_op jit(solution)/shard_map/dot_general | solution.py:58
  48.8 12.4 %fusion.8 = f32[64,4096]{1,0:T(8,128)S(1)} fusion(bf16[1,4096,3072]{2,1,0:T(8,128)(2,1)} %param.13, bf16[8,8,3072]{2,1,0:T(8,128)(2,1)S(1)} %all-to-all-done), kind=kOutput, calls=%fused_computation.10 | convolution fusion | flops 1610612736 | bytes 26607616 | tf_op jit(solution)/shard_map/dot_general | solution.py:62
  61.2 13.3 %fusion.4 = f32[64,3072]{1,0:T(8,128)} fusion(bf16[1,3072,4096]{2,1,0:T(8,128)(2,1)} %param.12, f32[64,4096]{1,0:T(8,128)S(1)} %fusion.8, f32[64,4096]{1,0:T(8,128)S(1)} %fusion.2), kind=kOutput, calls=%fused_computation.6 | convolution fusion | flops 1612185600 | bytes 28049408 | tf_op jit(solution)/shard_map/dot_general | solution.py:68
  74.5 20.9 %fusion.39 = bf16[8,8,3072]{2,1,0:T(8,128)(2,1)} fusion(f32[64,3072]{1,0:T(8,128)} %fusion.4, bf16[1,3072,4096]{2,1,0:T(8,128)(2,1)} %param.11, f32[64,4096]{1,0:T(8,128)S(1)} %fusion.8, bf16[1,3072,4096]{2,1,0:T(8,128)(2,1)} %param.12, f32[64,4096]{1,0:T(8,128)S(1)} %fusion.2, bf16[8,1,8,3072]{3,2,0,1:T(8,128)(2,1)S(1)} %constant_dynamic-update-slice_fusion, ...), kind=kOutput, calls=%fused_computation.19 | convolution fusion | flops 3224436736 | bytes 54001920 | tf_op jit(solution)/shard_map/dot_general | solution.py:67
  95.5 5.2 %all-to-all-start.2 = ((bf16[8,8,3072]{2,1,0:T(8,128)(2,1)}), bf16[8,8,3072]{2,1,0:T(8,128)(2,1)S(1)}, u32[]{:S(2)}, u32[]{:S(2)}) async-start(bf16[8,8,3072]{2,1,0:T(8,128)(2,1)} %fusion.39), calls=%async_computation.2 | async-start | bytes 786432 | tf_op jit(solution)/shard_map/all_to_all | solution.py:132
  100.7 8.7 %all-to-all-done.2 = bf16[8,8,3072]{2,1,0:T(8,128)(2,1)S(1)} async-done(((bf16[8,8,3072]{2,1,0:T(8,128)(2,1)}), bf16[8,8,3072]{2,1,0:T(8,128)(2,1)S(1)}, u32[]{:S(2)}, u32[]{:S(2)}) %all-to-all-start.2) | async-done | bytes 393248 | tf_op jit(solution)/shard_map/all_to_all | solution.py:132
  109.5 1.2 gather_fusion
  110.7 0.0 copy-start.3
  110.7 2.3 %gather_fusion.1 = f32[128,3072]{1,0:T(8,128)} fusion(f32[8,3072]{1,0:T(8,128)S(1)} %get-tuple-element.25, s32[1024]{0:T(1024)S(1)} %pad_clamp_fusion), kind=kCustom, calls=%fused_computation.1 | custom fusion | bytes 3146240 | tf_op jit(solution)/shard_map/gather | solution.py:136
  113.0 1.9 %fusion.52 = bf16[1,128,3072]{2,1,0:T(8,128)(2,1)S(1)} fusion(bf16[1,128,3072]{2,1,0:T(8,128)(2,1)S(1)} %copy-done.3, f32[128,3072]{1,0:T(8,128)} %gather_fusion.1, f32[128,3072]{1,0:T(8,128)S(1)} %gather_fusion, pred[128]{0:T(512)(128)(4,1)S(1)} %get-tuple-element.14, pred[128]{0:T(512)(128)(4,1)S(1)} %get-tuple-element.26), kind=kLoop, calls=%fused_computation.34 | loop fusion | flops 2359296 | bytes 4718848 | tf_op jit(solution)/shard_map/convert_element_type | solution.py:138
  114.9 7.0 %collective-permute-start.7 = (bf16[1,128,3072]{2,1,0:T(8,128)(2,1)S(1)}, bf16[1,128,3072]{2,1,0:T(8,128)(2,1)S(1)}, u32[]{:S(2)}, u32[]{:S(2)}) collective-permute-start(bf16[1,128,3072]{2,1,0:T(8,128)(2,1)S(1)} %fusion.52), channel_id=1, source_target_pairs={{8,0},{16,8},{24,16},{9,1},{17,9},{25,17},{10,2},{18,10},{26,18},{... | collective-permute-start | bytes 2359304 | tf_op jit(solution)/shard_map/ppermute | solution.py:54
  121.9 10.8 %collective-permute-done.7 = bf16[1,128,3072]{2,1,0:T(8,128)(2,1)S(1)} collective-permute-done((bf16[1,128,3072]{2,1,0:T(8,128)(2,1)S(1)}, bf16[1,128,3072]{2,1,0:T(8,128)(2,1)S(1)}, u32[]{:S(2)}, u32[]{:S(2)}) %collective-permute-start.7) | collective-permute-done | bytes 786464 | tf_op jit(solution)/shard_map/ppermute | solution.py:54
  132.7 0.9 copy.26
  (28 shorter events, 0.3 us)
Async XLA Ops:
  0.0 10.9 %copy-start = (bf16[1,128,3072]{2,1,0:T(8,128)(2,1)S(1)}, bf16[1,128,3072]{2,1,0:T(8,128)(2,1)}, u32[]{:S(2)}) copy-start(bf16[1,128,3072]{2,1,0:T(8,128)(2,1)} %param.7) | copy-start | bytes 2359300
  1.0 11.9 %copy-start.4 = (f32[1,128,2]{1,2,0:T(2,128)S(1)}, f32[1,128,2]{1,2,0:T(2,128)}, u32[]{:S(2)}) copy-start(f32[1,128,2]{1,2,0:T(2,128)} %param.10) | copy-start | bytes 3076
  3.9 11.6 %all-to-all-start.1 = ((s32[8,1,1]{2,1,0:T(1,128)}), s32[8,1,1]{2,1,0:T(1,128)S(1)}, u32[]{:S(2)}, u32[]{:S(2)}) async-start(s32[8,1,1]{2,1,0:T(1,128)} %all_to_all.16), calls=%async_computation.1 | async-start | bytes 8192 | tf_op jit(solution)/shard_map/all_to_all | solution.py:119
  10.3 2.9 %copy-start.2 = (bf16[1,128,3072]{2,1,0:T(8,128)(2,1)S(1)}, bf16[1,128,3072]{2,1,0:T(8,128)(2,1)}, u32[]{:S(2)}) copy-start(bf16[1,128,3072]{2,1,0:T(8,128)(2,1)} %param.8) | copy-start | bytes 2359300
  11.4 8.6 %collective-permute-start = (bf16[1,1,8,3072]{3,2,0,1:T(8,128)(2,1)S(1)}, bf16[1,1,8,3072]{3,2,0,1:T(8,128)(2,1)S(1)}, u32[]{:S(2)}, u32[]{:S(2)}) collective-permute-start(bf16[1,1,8,3072]{3,2,0,1:T(8,128)(2,1)S(1)} %constant_dynamic-slice_fusion.6), channel_id=1, source_target_pairs={{0,1},{1,2},{2,3},{3,4},{4,5},{5,6},{6,7},{7,0},{8,9},{9,10},{10,1... | collective-permute-start | bytes 147464 | tf_op jit(solution)/shard_map/ppermute | solution.py:42
  16.3 32.5 %all-to-all-start = ((bf16[8,8,3072]{2,1,0:T(8,128)(2,1)}), bf16[8,8,3072]{2,1,0:T(8,128)(2,1)S(1)}, u32[]{:S(2)}, u32[]{:S(2)}) async-start(bf16[8,8,3072]{2,1,0:T(8,128)(2,1)} %bitcast.5), calls=%async_computation | async-start | bytes 786432 | tf_op jit(solution)/shard_map/all_to_all | solution.py:118
  20.1 9.9 %collective-permute-start.1 = (bf16[1,1,8,3072]{3,2,0,1:T(8,128)(2,1)S(1)}, bf16[1,1,8,3072]{3,2,0,1:T(8,128)(2,1)S(1)}, u32[]{:S(2)}, u32[]{:S(2)}) collective-permute-start(bf16[1,1,8,3072]{3,2,0,1:T(8,128)(2,1)S(1)} %get-tuple-element.22), channel_id=1, source_target_pairs={{0,2},{1,3},{2,4},{3,5},{4,6},{5,7},{6,0},{7,1},{8,10},{9,11},{10,... | collective-permute-start | bytes 147464 | tf_op jit(solution)/shard_map/ppermute | solution.py:42
  22.5 15.7 %collective-permute-start.6 = (bf16[1,1,8,3072]{3,2,0,1:T(8,128)(2,1)S(1)}, bf16[1,1,8,3072]{3,2,0,1:T(8,128)(2,1)S(1)}, u32[]{:S(2)}, u32[]{:S(2)}) collective-permute-start(bf16[1,1,8,3072]{3,2,0,1:T(8,128)(2,1)S(1)} %get-tuple-element.17), channel_id=1, source_target_pairs={{0,7},{1,0},{2,1},{3,2},{4,3},{5,4},{6,5},{7,6},{8,15},{9,8},{10,9... | collective-permute-start | bytes 147464 | tf_op jit(solution)/shard_map/ppermute | solution.py:42
  24.6 13.6 %collective-permute-start.5 = (bf16[1,1,8,3072]{3,2,0,1:T(8,128)(2,1)S(1)}, bf16[1,1,8,3072]{3,2,0,1:T(8,128)(2,1)S(1)}, u32[]{:S(2)}, u32[]{:S(2)}) collective-permute-start(bf16[1,1,8,3072]{3,2,0,1:T(8,128)(2,1)S(1)} %get-tuple-element.18), channel_id=1, source_target_pairs={{0,6},{1,7},{2,0},{3,1},{4,2},{5,3},{6,4},{7,5},{8,14},{9,15},{10,... | collective-permute-start | bytes 147464 | tf_op jit(solution)/shard_map/ppermute | solution.py:42
  25.8 12.4 %collective-permute-start.4 = (bf16[1,1,8,3072]{3,2,0,1:T(8,128)(2,1)S(1)}, bf16[1,1,8,3072]{3,2,0,1:T(8,128)(2,1)S(1)}, u32[]{:S(2)}, u32[]{:S(2)}) collective-permute-start(bf16[1,1,8,3072]{3,2,0,1:T(8,128)(2,1)S(1)} %get-tuple-element.19), channel_id=1, source_target_pairs={{0,5},{1,6},{2,7},{3,0},{4,1},{5,2},{6,3},{7,4},{8,13},{9,14},{10,... | collective-permute-start | bytes 147464 | tf_op jit(solution)/shard_map/ppermute | solution.py:42
  26.1 12.1 %collective-permute-start.3 = (bf16[1,1,8,3072]{3,2,0,1:T(8,128)(2,1)S(1)}, bf16[1,1,8,3072]{3,2,0,1:T(8,128)(2,1)S(1)}, u32[]{:S(2)}, u32[]{:S(2)}) collective-permute-start(bf16[1,1,8,3072]{3,2,0,1:T(8,128)(2,1)S(1)} %get-tuple-element.20), channel_id=1, source_target_pairs={{0,4},{1,5},{2,6},{3,7},{4,0},{5,1},{6,2},{7,3},{8,12},{9,13},{10,... | collective-permute-start | bytes 147464 | tf_op jit(solution)/shard_map/ppermute | solution.py:42
  30.0 8.2 %collective-permute-start.2 = (bf16[1,1,8,3072]{3,2,0,1:T(8,128)(2,1)S(1)}, bf16[1,1,8,3072]{3,2,0,1:T(8,128)(2,1)S(1)}, u32[]{:S(2)}, u32[]{:S(2)}) collective-permute-start(bf16[1,1,8,3072]{3,2,0,1:T(8,128)(2,1)S(1)} %get-tuple-element.21), channel_id=1, source_target_pairs={{0,3},{1,4},{2,5},{3,6},{4,7},{5,0},{6,1},{7,2},{8,11},{9,12},{10,... | collective-permute-start | bytes 147464 | tf_op jit(solution)/shard_map/ppermute | solution.py:42
  95.5 13.9 %all-to-all-start.2 = ((bf16[8,8,3072]{2,1,0:T(8,128)(2,1)}), bf16[8,8,3072]{2,1,0:T(8,128)(2,1)S(1)}, u32[]{:S(2)}, u32[]{:S(2)}) async-start(bf16[8,8,3072]{2,1,0:T(8,128)(2,1)} %fusion.39), calls=%async_computation.2 | async-start | bytes 786432 | tf_op jit(solution)/shard_map/all_to_all | solution.py:132
  110.7 2.3 %copy-start.3 = (bf16[1,128,3072]{2,1,0:T(8,128)(2,1)S(1)}, bf16[1,128,3072]{2,1,0:T(8,128)(2,1)}, u32[]{:S(2)}) copy-start(bf16[1,128,3072]{2,1,0:T(8,128)(2,1)} %param.8) | copy-start | bytes 2359300
  113.0 20.6 %copy-start.1 = (bf16[1,128,3072]{2,1,0:T(8,128)(2,1)S(1)}, bf16[1,128,3072]{2,1,0:T(8,128)(2,1)}, u32[]{:S(2)}) copy-start(bf16[1,128,3072]{2,1,0:T(8,128)(2,1)} %param.7) | copy-start | bytes 2359300
  114.9 17.8 %collective-permute-start.7 = (bf16[1,128,3072]{2,1,0:T(8,128)(2,1)S(1)}, bf16[1,128,3072]{2,1,0:T(8,128)(2,1)S(1)}, u32[]{:S(2)}, u32[]{:S(2)}) collective-permute-start(bf16[1,128,3072]{2,1,0:T(8,128)(2,1)S(1)} %fusion.52), channel_id=1, source_target_pairs={{8,0},{16,8},{24,16},{9,1},{17,9},{25,17},{10,2},{18,10},{26,18},{... | collective-permute-start | bytes 2359304 | tf_op jit(solution)/shard_map/ppermute | solution.py:54
